TPU v7x, 32 devices: a whole 2x2x4 slice. The times are simulated.
32 devices in a mesh: depth: 4 (over y, x), tile: 8 (over z, core).
Axes of the slice: x: 2, y: 2, z: 4, core: 2. Of those that a mesh axis runs over, the one named last changes fastest.
Arguments:
- density: bfloat16 [128, 512, 2048], P('depth', 'tile'), may hold values from 0 to 2
- depth_rank: int32 [4], replicated, may hold values from 0 to 3, as said below
- piece_home: int32 [64], P('tile'), may hold values from 0 to 63, as said below
Outputs:
- display: float32 [3, 4, 64, 4096], P(None, 'depth', 'tile')
Inputs may be any that keep to these rules, and one draw needn't show every extreme that they name: Either depth_rank[i] = i for every i, or depth_rank[i] = 3 - i for every i. `piece_home`: every value appears exactly once. A value h names slot h % 8 of the device h // 8 along tile. The number of the 8 entries of tile device s that name device o depends only on (o - s) mod 8, is at most 2, and equals 2 for some pair.
All inputs are finite; a program needn't handle non-finite values.
Results may differ from a plain program's by a relative error of at most 0.0003.
Values may be sent and summed in bfloat16 or wider, within the bound.
A program may use at most 128 MiB of HBM per device.

v0:
```python
import math
import jax
import jax.numpy as jnp
import numpy as np
from jax import lax
from jax.experimental import pallas as pl
from jax.experimental.pallas import tpu as pltpu
from jax.sharding import PartitionSpec as P

MOST = 2
EMPTY = -(2**30)

EXTINCT = 0.5
LIGHT_Z = 0.6
LIGHT_Y = 0.48
LIGHT_X = 0.64
SHARPNESS = 6.0
BACKDROP = (0.08, 0.1, 0.14)

PAD = 128
CB = 256
MC = 128
SIG_A = math.exp(-3.0)
SIG_B = math.exp(-2.5)
SIN = (0.9999999978529928,
       -0.1666666388441264,
       0.008333274854744043,
       -0.00019836767087186654,
       2.7400072109094996e-06,
       -2.2499595606831132e-08)


def inverse(x):
    return 1.0 / x


def stencils(rows):
    wy, wz = LIGHT_Y / LIGHT_X, LIGHT_Z / LIGHT_X
    left = np.zeros((rows, 3 * rows), np.float32)
    for r in range(rows):
        left[r, r] = -wz
        left[r, 2 * rows + r] = wz
        if r < rows - 1:
            left[r, rows + r + 1] = wy
        if r > 0:
            left[r, rows + r - 1] = -wy
    right = np.zeros((CB + 2 * PAD, CB), np.float32)
    for c in range(CB):
        right[c + PAD + 1, c] = 1.0
        right[c + PAD - 1, c] = -1.0
    return jnp.asarray(left, jnp.bfloat16), jnp.asarray(right, jnp.bfloat16)


def make_facing(d, g_pair, dens_pair, hs, left, right, cells, rows, zc):
    wy = LIGHT_Y / LIGHT_X

    def facing(block, slot, chunk):
        z0 = chunk * zc
        g, dens32 = g_pair[slot], dens_pair[slot]
        c0 = pl.multiple_of(block * CB, CB)
        wide = d[pl.ds(z0 + 1, zc), :, pl.ds(c0, CB + 2 * PAD)]
        dx = jnp.dot(wide.reshape(zc * rows, CB + 2 * PAD), right[...],
                     preferred_element_type=jnp.float32)
        c1 = pl.multiple_of(block * CB + PAD, PAD)
        sub = lax.broadcasted_iota(jnp.int32, (8, CB), 0)
        for i in range(zc):
            tall = d[pl.ds(z0 + i, 3), :, pl.ds(c1, CB)].reshape(3 * rows, CB)
            dyz = jnp.dot(left[...], tall, preferred_element_type=jnp.float32)
            both = dyz + dx[i * rows:(i + 1) * rows]
            low = hs[0, pl.ds(z0 + i, 1), :] * wy
            high = hs[1, pl.ds(z0 + i, 1), :] * wy
            g[z0 + i, 0:8] = both[0:8] - jnp.where(sub == 0, low, 0.0)
            g[z0 + i, 8:rows - 8] = both[8:rows - 8]
            g[z0 + i, rows - 8:rows] = both[rows - 8:] + jnp.where(sub == 7, high, 0.0)
            dens32[z0 + i] = wide[i, :, PAD:PAD + CB].astype(jnp.float32)

    return facing


def march(dens32, g, state, ascend, band, half, halves, cells, c0):
    steps = cells // halves
    first = half == 0
    lanes = slice(c0, c0 + MC)
    trans = jnp.where(first, 1.0, state[0, :, lanes])
    total, m0, m1, wave = (jnp.where(first, 0.0, state[i, :, lanes]) for i in range(1, 5))
    band_rows = state.shape[1]
    r0 = pl.multiple_of(band * band_rows, 8)
    bias = (0.35 + 0.65 * 0.5) / (0.65 * 0.5)
    for i in range(steps):
        k = half * steps + i
        z = jnp.where(ascend, k, cells - 1 - k)
        dens = dens32[z, pl.ds(r0, band_rows), lanes]
        face = g[z, pl.ds(r0, band_rows), lanes]
        shade = jnp.tanh(face * (0.5 * SHARPNESS * LIGHT_X)) + bias
        after = trans * jnp.exp2(dens * (-EXTINCT * math.log2(math.e)))
        ws = (trans - after) * shade
        trans = after
        u = dens + 0.01
        wr = ws * inverse((u + SIG_A) * (u + SIG_B))
        y = jnp.log(u) * (1.7 / 2) + math.pi / 2
        q = y * y
        c = SIN[-1]
        for coef in SIN[-2::-1]:
            c = c * q + coef
        c = c * y
        total = total + ws
        m0 = m0 + wr
        m1 = m1 + wr * u
        wave = wave + ws * (c * c)
    for i, val in enumerate((trans, total, m0, m1, wave)):
        state[i, :, lanes] = val
    scale = 0.65 * 0.5
    return (
        scale * (total - SIG_A * (m1 + SIG_B * m0)),
        scale * wave,
        scale * SIG_B * (m1 + SIG_A * m0),
        trans,
    )


def brick_kernel(nd, nt, pieces, rank, route, dens, ylast, yfirst, labels, left, right, inbox, arrived,
                 d, hb, hs, g0, g1, dens0, dens1, state, out, recv, fin, outbox,
                 dens_sem, hsend, hrecv, dsend, drecv, tsend, trecv, lsend, lrecv):
    cells, rows, cols = dens.shape
    nb, halves = cols // CB, 2
    its = nd * halves
    zc = cells // its
    qrows = rows // nd
    width, rpp = outbox.shape[3], outbox.shape[2] // MOST
    groups = tsend.shape[0]
    me_d, me_t = lax.axis_index("depth"), lax.axis_index("tile")
    mesh_ids = pl.DeviceIdType.MESH

    barrier = pltpu.get_barrier_semaphore()

    @pl.loop(1, nt)
    def _(o):
        pl.semaphore_signal(barrier, inc=1, device_id=(me_d, lax.rem(me_t + o, nt)), device_id_type=mesh_ids)

    for k in range(1, nd):
        pl.semaphore_signal(barrier, inc=1, device_id=(lax.rem(me_d + k, nd), me_t), device_id_type=mesh_ids)

    def cols_of(b):
        return pl.ds(pl.multiple_of(b * CB, CB), CB)

    def pads_of(b):
        return pl.ds(pl.multiple_of(b * CB + PAD, PAD), CB)

    def dens_copy(b):
        return pltpu.make_async_copy(
            dens.at[:, :, cols_of(b)], d.at[pl.ds(1, cells), :, pads_of(b)], dens_sem.at[b])

    def halo(kind, b):
        src, dst, step = (
            (dens.at[cells - 1, :, cols_of(b)], d.at[0, :, pads_of(b)], 1),
            (dens.at[0, :, cols_of(b)], d.at[cells + 1, :, pads_of(b)], nd - 1),
            (ylast.at[:, cols_of(b)], hb.at[0, :, cols_of(b)], 1),
            (yfirst.at[:, cols_of(b)], hb.at[1, :, cols_of(b)], nt - 1),
        )[kind]
        to = (lax.rem(me_d + step, nd), me_t) if kind < 2 else (me_d, lax.rem(me_t + step, nt))
        return pltpu.make_async_remote_copy(
            src_ref=src, dst_ref=dst, send_sem=hsend.at[kind, b], recv_sem=hrecv.at[kind, b],
            device_id=to, device_id_type=mesh_ids)

    sends = (me_d < nd - 1, me_d > 0, me_t < nt - 1, me_t > 0)
    gets = (me_d > 0, me_d < nd - 1, me_t > 0, me_t < nt - 1)

    @pl.loop(0, nb)
    def _(b):
        dens_copy(b).start()

    side = jnp.zeros((cells + 2, rows, PAD), d.dtype)
    d[:, :, :PAD] = side
    d[:, :, cols + PAD:] = side

    @pl.when(me_d == 0)
    def _():
        d[0, :, PAD:cols + PAD] = jnp.zeros((rows, cols), d.dtype)

    @pl.when(me_d == nd - 1)
    def _():
        d[cells + 1, :, PAD:cols + PAD] = jnp.zeros((rows, cols), d.dtype)

    @pl.when(me_t == 0)
    def _():
        hb[0] = jnp.zeros((cells, cols), hb.dtype)

    @pl.when(me_t == nt - 1)
    def _():
        hb[1] = jnp.zeros((cells, cols), hb.dtype)

    pl.semaphore_wait(barrier, nt - 1 + nd - 1)

    @pl.loop(0, nb)
    def _(b):
        for kind in range(4):
            @pl.when(sends[kind])
            def _():
                halo(kind, b).start()

    def label_copy(o):
        return pltpu.make_async_remote_copy(
            src_ref=labels.at[o], dst_ref=arrived.at[o], send_sem=lsend.at[o], recv_sem=lrecv.at[o],
            device_id=(me_d, lax.rem(me_t + o, nt)), device_id_type=mesh_ids)

    own_labels = pltpu.make_async_copy(labels.at[0], arrived.at[0], lsend.at[0])
    own_labels.start()

    @pl.loop(1, nt)
    def _(o):
        label_copy(o).start()

    def arrive(b):
        dens_copy(b).wait()
        for kind in range(4):
            @pl.when(gets[kind])
            def _():
                halo(kind, b).wait_recv()

    def spread(b):
        hs[...] = hb[:, :, cols_of(b)].astype(jnp.float32)

    ascend = rank[0] == 0
    g_pair, dens_pair = (g0, g1), (dens0, dens1)
    facing = make_facing(d, g_pair, dens_pair, hs, left, right, cells, rows, zc)

    def depth_copy(k, b, src):
        to = lax.rem(me_d + k, nd)
        return pltpu.make_async_remote_copy(
            src_ref=out.at[:, pl.ds(pl.multiple_of(to * qrows, 8), qrows), cols_of(b)],
            dst_ref=recv.at[src, :, :, cols_of(b)],
            send_sem=dsend.at[b, k], recv_sem=drecv.at[b, src],
            device_id=(to, me_t), device_id_type=mesh_ids)

    def keep_own(b):
        mine = out[:, pl.ds(pl.multiple_of(me_d * qrows, 8), qrows), cols_of(b)]
        recv[me_d, :, :, cols_of(b)] = mine

    def composite(b):
        for k in range(1, nd):
            depth_copy(k, b, lax.rem(me_d + k, nd)).wait_recv()
        color = recv[0, 0:3, :, cols_of(b)]
        trans = recv[0, 3, :, cols_of(b)]
        for i in range(1, nd):
            new = recv[i, 0:3, :, cols_of(b)]
            new_trans = recv[i, 3, :, cols_of(b)]
            front, back = jnp.where(ascend, color, new), jnp.where(ascend, new, color)
            color = front + jnp.where(ascend, trans, new_trans)[None] * back
            trans = trans * new_trans
        for ch in range(3):
            fin[ch, :, cols_of(b)] = color[ch] + trans * BACKDROP[ch]

    def tile_copy(o, part, window):
        return pltpu.make_async_remote_copy(
            src_ref=outbox.at[o, :, :, window], dst_ref=inbox.at[o, :, :, window],
            send_sem=tsend.at[part, o], recv_sem=trecv.at[part, o],
            device_id=(me_d, lax.rem(me_t + o, nt)), device_id_type=mesh_ids)

    def tile_own(part, window):
        return pltpu.make_async_copy(
            outbox.at[0, :, :, window], inbox.at[0, :, :, window], tsend.at[part, 0])

    def ship(part, window):
        @pl.loop(0, nt)
        def _(o):
            for m in range(MOST):
                p = lax.div((2 * m - 1) * route[o, 0, m], pieces)
                p = jnp.where(route[o, 0, m] == EMPTY, 0, p)
                for r in range(rpp):
                    if width == cols:
                        piece = fin[:, pl.ds(p * rpp + r, 1), window]
                    else:
                        per = cols // width
                        c = pl.multiple_of(lax.rem(p, per) * width, width)
                        piece = fin[:, pl.ds(lax.div(p, per), 1), pl.ds(c, width)]
                    outbox[o, :, m * rpp + r:m * rpp + r + 1, window] = piece

        tile_own(part, window).start()

        @pl.loop(1, nt)
        def _(o):
            tile_copy(o, part, window).start()

    arrive(0)
    arrive(1)
    spread(0)

    @pl.loop(0, its)
    def _(it):
        facing(0, 0, it)

    def finish(b):
        composite(b)
        if groups == nb:
            ship(b, cols_of(b))

    def step(b, slot):
        @pl.when(b + 2 < nb)
        def _():
            arrive(b + 2)

        ahead = lax.rem(b + 1, nb)
        spread(ahead)

        @pl.loop(0, its)
        def _(it):
            facing(ahead, 1 - slot, it)
            k = lax.div(it, halves) + 1
            half = lax.rem(it, halves)
            band = lax.rem(me_d + k, nd)
            for c0 in range(0, CB, MC):
                vals = march(dens_pair[slot], g_pair[slot], state, ascend, band, half, halves, cells, c0)
                lanes = pl.ds(pl.multiple_of(b * CB + c0, MC), MC)
                for ch, val in enumerate(vals):
                    out[ch, pl.ds(pl.multiple_of(band * qrows, 8), qrows), lanes] = val

            @pl.when((half == halves - 1) & (k < nd))
            def _():
                depth_copy(k, b, me_d).start()

        keep_own(b)

        @pl.when(b > 0)
        def _():
            finish(b - 1)

    @pl.loop(0, nb // 2)
    def _(pair):
        step(2 * pair, 0)
        step(2 * pair + 1, 1)

    finish(nb - 1)
    if groups != nb:
        ship(0, pl.ds(0, width))

    own_labels.wait()

    @pl.loop(1, nt)
    def _(o):
        label_copy(o).wait()

    @pl.loop(0, groups)
    def _(part):
        window = cols_of(part) if groups == nb else pl.ds(0, width)
        tile_own(part, window).wait()

        @pl.loop(1, nt)
        def _(o):
            tile_copy(o, part, window).wait()

    @pl.loop(0, nb)
    def _(b):
        for k in range(1, nd):
            depth_copy(k, b, me_d).wait_send()

    for kind in range(4):
        @pl.when(sends[kind])
        def _():
            @pl.loop(0, nb)
            def _(b):
                halo(kind, b).wait_send()


def place_kernel(arrived, inbox, display):
    nt, rpp, width = inbox.shape[0], inbox.shape[2] // MOST, inbox.shape[3]

    @pl.loop(0, nt)
    def _(o):
        for m in range(MOST):
            value = (2 * m - 1) * arrived[o, 0, m]
            label = lax.rem(value, display.shape[2])
            here = arrived[o, 0, m] != EMPTY
            if m:
                here = here & (value != -arrived[o, 0, 0])

            @pl.when(here)
            def _():
                for r in range(rpp):
                    piece = inbox[o, :, m * rpp + r:m * rpp + r + 1, :]
                    display[:, 0, pl.ds(label, 1), r * width:(r + 1) * width] = piece


def on_device(density, depth_rank, piece_home):
    cells, rows, cols = density.shape
    nd, nt = lax.axis_size("depth"), lax.axis_size("tile")
    ppd = piece_home.shape[0]
    qrows = rows // nd
    piece_len = qrows * cols // ppd
    width = min(piece_len, cols)
    rpp = piece_len // width
    nb = cols // CB
    groups = nb if width == cols else 1

    order = jnp.arange(ppd, dtype=jnp.int32)
    owners = piece_home // ppd
    code = order * ppd + piece_home % ppd
    offset = (owners - lax.axis_index("tile") + nt) % nt
    signs = jnp.where(jnp.arange(128) == 0, -1, 1)[None, None, :, None]
    goes = offset[None, None, None, :] == jnp.arange(nt)[:, None, None, None]
    codes = jnp.max(jnp.where(goes, signs * code[None, None, None, :], EMPTY), axis=3)
    ylast, yfirst = density[:, rows - 1], density[:, 0]
    left, right = stencils(rows)
    anyspec = pl.BlockSpec(memory_space=pl.ANY)
    vmem = pl.BlockSpec(memory_space=pltpu.VMEM)
    smem = pl.BlockSpec(memory_space=pltpu.SMEM)
    dma = pltpu.SemaphoreType.DMA
    f32 = jnp.float32
    inbox, arrived = pl.pallas_call(
        lambda *refs: brick_kernel(nd, nt, ppd, *refs),
        out_shape=(jax.ShapeDtypeStruct((nt, 3, MOST * rpp, width), f32),
                   jax.ShapeDtypeStruct((nt, 1, 128), jnp.int32)),
        in_specs=[smem, smem] + [anyspec] * 4 + [vmem] * 2,
        out_specs=(anyspec, anyspec),
        scratch_shapes=[
            pltpu.VMEM((cells + 2, rows, cols + 2 * PAD), jnp.bfloat16),
            pltpu.VMEM((2, cells, cols), jnp.bfloat16),
            pltpu.VMEM((2, cells, CB), f32),
            pltpu.VMEM((cells, rows, CB), f32),
            pltpu.VMEM((cells, rows, CB), f32),
            pltpu.VMEM((cells, rows, CB), f32),
            pltpu.VMEM((cells, rows, CB), f32),
            pltpu.VMEM((5, qrows, CB), f32),
            pltpu.VMEM((4, rows, cols), f32),
            pltpu.VMEM((nd, 4, qrows, cols), f32),
            pltpu.VMEM((3, qrows, cols), f32),
            pltpu.VMEM((nt, 3, MOST * rpp, width), f32),
            dma((nb,)), dma((4, nb)), dma((4, nb)), dma((nb, nd)), dma((nb, nd)),
            dma((groups, nt)), dma((groups, nt)), dma((nt,)), dma((nt,)),
        ],
        compiler_params=pltpu.CompilerParams(
            collective_id=0, has_side_effects=True, vmem_limit_bytes=56 * 1024 * 1024),
    )(depth_rank, codes, density, ylast, yfirst, codes, left, right)
    return pl.pallas_call(
        place_kernel,
        out_shape=jax.ShapeDtypeStruct((3, 1, ppd, piece_len), f32),
        in_specs=[smem, vmem],
        out_specs=vmem,
    )(arrived, inbox)


def solution(mesh):
    in_specs = (P("depth", "tile", None), P(), P("tile"))
    out_specs = P(None, "depth", "tile", None)
    return jax.shard_map(
        on_device, mesh=mesh, in_specs=in_specs, out_specs=out_specs, check_vma=False
    )
```

profile of v0, /device:TPU:0, one launch (start us, length us, event | category | flops | bytes accessed | tf_op | source)
XLA Modules:
  0.0 67.1 jit_solution(10684888701375588054)
XLA Ops:
  0.0 0.7 %and_select_fusion.1 = (s32[8]{0:T(128)S(1)}, s32[8]{0:T(128)S(1)}) fusion(s32[8]{0:T(128)} %param.7, s32[]{:T(128)S(6)} %axis_index.12), kind=kLoop, calls=%fused_computation.9 | loop fusion | flops 272 | bytes 100 | tf_op jit(solution)/shard_map/jit(remainder)/select_n | solution.py:397
  0.7 0.1 broadcast_multiply_fusion
  0.8 0.7 %select_reduce_fusion = s32[8,128]{1,0:T(8,128)} fusion(s32[128,8]{0,1:T(8,128)S(1)} %broadcast_multiply_fusion, pred[8,8]{1,0:T(8,128)(4,1)S(1)} %iota_compare_fusion), kind=kLoop, calls=%fused_computation.2 | loop fusion | flops 15360 | bytes 8256 | tf_op jit(solution)/shard_map/reduce_max | solution.py:400
  1.4 2.0 %fusion.2 = (bf16[32,1,2048]{2,1,0:T(2,128)(2,1)S(1)}, bf16[32,1,2048]{2,1,0:T(2,128)(2,1)S(1)}) fusion(bf16[32,64,2048]{2,1,0:T(8,128)(2,1)} %refs_2_.1), kind=kLoop, calls=%fused_computation.16 | loop fusion | bytes 524288 | tf_op jit(solution)/shard_map/slice | solution.py:401
  3.4 0.8 %copy_bitcast_fusion = (bf16[32,2048]{1,0:T(8,128)(2,1)}, bf16[32,2048]{1,0:T(8,128)(2,1)}) fusion(bf16[32,1,2048]{2,1,0:T(2,128)(2,1)S(1)} %get-tuple-element.9, bf16[32,1,2048]{2,1,0:T(2,128)(2,1)S(1)} %get-tuple-element.10), kind=kLoop, calls=%fused_computation | loop fusion | bytes 524288 | tf_op jit(solution)/shard_map/squeeze | solution.py:401
  4.3 60.6 %shard_map.55 = (f32[8,3,4,2048]{3,2,1,0:T(4,128)}, s32[8,1,128]{2,1,0:T(1,128)}) custom-call(s32[4]{0:T(128)} %refs_0_.1, s32[8,1,128]{2,1,0:T(1,128)} %bitcast.5, bf16[32,64,2048]{2,1,0:T(8,128)(2,1)} %refs_2_.1, bf16[32,2048]{1,0:T(8,128)(2,1)} %get-tuple-element.14.refs_3_, bf16[32,2048]{1,0:T(8,128)(2,1)} %get-tuple-element.13.refs_4_, ...), custom_call_target="tpu_custom_call" | custom-call | tf_op jit(solution)/shard_map/pallas_call | solution.py:408
  64.9 2.2 %shard_map.56 = f32[3,1,8,4096]{3,2,1,0:T(8,128)} custom-call(s32[8,1,128]{2,1,0:T(1,128)} %get-tuple-element.7.arrived, f32[8,3,4,2048]{3,2,1,0:T(4,128)} %get-tuple-element.8.inbox), custom_call_target="tpu_custom_call" | custom-call | tf_op jit(solution)/shard_map/pallas_call | solution.py:433
  (2 shorter events, 0.0 us)
where the time goes:
time: 67.2 us; the launch traced here: 67.1 us
  Pallas kernels  62.8 us (93%)
  local copies, waits for them, and re-layouts  2.82 us (4%)
  other arithmetic  1.44 us (2%)
    pallas_call x1, Pallas kernels, on_device(): pl.pallas_call(lambda *refs: brick_kernel(nd, nt, ppd, *refs), out_shape=...  60.6 us
    pallas_call x1, Pallas kernels, on_device(): pl.pallas_call(place_kernel, out_shape=jax.ShapeDtypeStruct((3, 1, ppd, p...  2.15 us
    slice x1, local copies, waits for them, and re-layouts, on_device(): ylast, yfirst = (density[:, rows - 1], density[:, 0])  1.97 us

commit v1 on v0

v1 whole, which is shorter than its diff:
```python
import math
import jax
import jax.numpy as jnp
import numpy as np
from jax import lax
from jax.experimental import pallas as pl
from jax.experimental.pallas import tpu as pltpu
from jax.sharding import PartitionSpec as P

MOST = 2
NONE = -1

EXTINCT = 0.5
LIGHT_Z = 0.6
LIGHT_Y = 0.48
LIGHT_X = 0.64
SHARPNESS = 6.0
BACKDROP = (0.08, 0.1, 0.14)

PAD = 128
CB = 256
MC = 128
EDGE = 8
SIG_A = math.exp(-3.0)
SIG_B = math.exp(-2.5)
SHIFT = math.pi / 2 / (0.85 * math.log(2))
LEAD = 6.138231308051623e-10
SINSQ = (141379137.46788317, -4089655.3240788155, 47304.237438791075, -291.0939487912164)
UNIT = 65535.0
LOW = 65535


def stencils(rows):
    wy, wz = LIGHT_Y / LIGHT_X, LIGHT_Z / LIGHT_X
    left = np.zeros((rows, 3 * rows + 2 * EDGE), np.float32)
    for r in range(rows):
        left[r, r] = -wz
        left[r, 2 * rows + 2 * EDGE + r] = wz
        if r < rows - 1:
            left[r, rows + r + 1] = wy
        if r > 0:
            left[r, rows + r - 1] = -wy
    left[0, 2 * rows + EDGE - 1] = -wy
    left[rows - 1, 2 * rows + EDGE] = wy
    right = np.zeros((CB + 2 * PAD, CB), np.float32)
    for c in range(CB):
        right[c + PAD + 1, c] = 1.0
        right[c + PAD - 1, c] = -1.0
    return jnp.asarray(left, jnp.bfloat16), jnp.asarray(right, jnp.bfloat16)


def make_facing(d, g_pair, dens_pair, left, right, rows, zc):
    def facing(block, slot, chunk):
        z0 = chunk * zc
        g, dens16 = g_pair[slot], dens_pair[slot]
        c0 = pl.multiple_of(block * CB, CB)
        c1 = pl.multiple_of(block * CB + PAD, PAD)
        wide = d[pl.ds(z0 + 1, zc), 0:rows, pl.ds(c0, CB + 2 * PAD)]
        dx = jnp.dot(wide.reshape(zc * rows, CB + 2 * PAD), right[...],
                     preferred_element_type=jnp.float32)
        dens16[pl.ds(z0, zc)] = wide[:, :, PAD:PAD + CB]
        for i in range(zc):
            tall = jnp.concatenate([
                d[z0 + i, 0:rows, pl.ds(c1, CB)],
                d[z0 + i + 1, :, pl.ds(c1, CB)],
                d[z0 + i + 2, 0:rows, pl.ds(c1, CB)]], axis=0)
            dyz = jnp.dot(left[...], tall, preferred_element_type=jnp.float32)
            g[z0 + i] = dyz + dx[i * rows:(i + 1) * rows]

    return facing


def march(dens16, g, ascend, r0, lanes, band_rows, cells):
    bias = (0.35 + 0.65 * 0.5) / (0.65 * 0.5)
    zero = jnp.zeros((band_rows, MC), jnp.float32)
    trans = zero + 1.0
    total = m0 = m1 = wave = zero
    for k in range(cells):
        z = jnp.where(ascend, k, cells - 1 - k)
        dens = dens16[z, pl.ds(r0, band_rows), lanes].astype(jnp.float32)
        face = g[z, pl.ds(r0, band_rows), lanes]
        shade = jnp.tanh(face * (0.5 * SHARPNESS * LIGHT_X)) + bias
        after = trans * jnp.exp2(dens * (-EXTINCT * math.log2(math.e)))
        ws = (trans - after) * shade
        trans = after
        v = jnp.log2(dens + 0.01) + SHIFT
        q = v * v
        c = q + SINSQ[-1]
        for coef in SINSQ[-2::-1]:
            c = c * q + coef
        c = c * q
        total = total + ws
        m0 = m0 + ws * (1.0 / (dens + (0.01 + SIG_A)))
        m1 = m1 + ws * (1.0 / (dens + (0.01 + SIG_B)))
        wave = wave + ws * (c * (1.0 / LEAD - c))
    scale = 0.65 * 0.5
    return (
        scale * (total - SIG_A * m0),
        (scale * 4 * LEAD * LEAD) * wave,
        (scale * SIG_B) * m1,
        trans,
    )


def coded(value):
    return jnp.clip(value + 0.5, 0.0, UNIT).astype(jnp.int32)


def join(low, high):
    return low | (high << 16)


def low_part(word):
    return (word & LOW).astype(jnp.float32)


def high_part(word):
    return lax.shift_right_logical(word, 16).astype(jnp.float32)


def brick_kernel(nd, nt, ppd, rank, home, dens, names, left, right, inbox, arrived,
                 d, g0, g1, dens0, dens1, out, recv, fin, outbox, route,
                 dens_sem, hsend, hrecv, dsend, drecv, tsend, trecv, lsend, lrecv):
    cells, rows, cols = dens.shape
    nb, parts = cols // CB, CB // MC
    its = nd * parts
    zc = cells // its
    qrows = rows // nd
    width, rpp = outbox.shape[3], outbox.shape[2]
    groups = tsend.shape[0]
    me_d, me_t = lax.axis_index("depth"), lax.axis_index("tile")
    mesh_ids = pl.DeviceIdType.MESH

    barrier = pltpu.get_barrier_semaphore()

    @pl.loop(1, nt)
    def _(o):
        pl.semaphore_signal(barrier, inc=1, device_id=(me_d, lax.rem(me_t + o, nt)), device_id_type=mesh_ids)

    for k in range(1, nd):
        pl.semaphore_signal(barrier, inc=1, device_id=(lax.rem(me_d + k, nd), me_t), device_id_type=mesh_ids)

    def cols_of(b):
        return pl.ds(pl.multiple_of(b * CB, CB), CB)

    def pads_of(b):
        return pl.ds(pl.multiple_of(b * CB + PAD, PAD), CB)

    def dens_copy(b):
        return pltpu.make_async_copy(
            dens.at[:, :, cols_of(b)], d.at[pl.ds(1, cells), pl.ds(0, rows), pads_of(b)], dens_sem.at[b])

    def halo(kind, b):
        inner = pl.ds(1, cells)
        src, dst, step = (
            (dens.at[cells - 1, :, cols_of(b)], d.at[0, pl.ds(0, rows), pads_of(b)], 1),
            (dens.at[0, :, cols_of(b)], d.at[cells + 1, pl.ds(0, rows), pads_of(b)], nd - 1),
            (dens.at[:, pl.ds(rows - EDGE, EDGE), cols_of(b)],
             d.at[inner, pl.ds(rows, EDGE), pads_of(b)], 1),
            (dens.at[:, pl.ds(0, EDGE), cols_of(b)],
             d.at[inner, pl.ds(rows + EDGE, EDGE), pads_of(b)], nt - 1),
        )[kind]
        to = (lax.rem(me_d + step, nd), me_t) if kind < 2 else (me_d, lax.rem(me_t + step, nt))
        return pltpu.make_async_remote_copy(
            src_ref=src, dst_ref=dst, send_sem=hsend.at[kind, b], recv_sem=hrecv.at[kind, b],
            device_id=to, device_id_type=mesh_ids)

    sends = (me_d < nd - 1, me_d > 0, me_t < nt - 1, me_t > 0)
    gets = (me_d > 0, me_d < nd - 1, me_t > 0, me_t < nt - 1)

    @pl.loop(0, nb)
    def _(b):
        dens_copy(b).start()

    side = jnp.zeros((cells + 2, rows + 2 * EDGE, PAD), d.dtype)
    d[:, :, :PAD] = side
    d[:, :, cols + PAD:] = side

    @pl.when(me_d == 0)
    def _():
        d[0, 0:rows, PAD:cols + PAD] = jnp.zeros((rows, cols), d.dtype)

    @pl.when(me_d == nd - 1)
    def _():
        d[cells + 1, 0:rows, PAD:cols + PAD] = jnp.zeros((rows, cols), d.dtype)

    edge = jnp.zeros((cells, EDGE, cols), d.dtype)

    @pl.when(me_t == 0)
    def _():
        d[1:cells + 1, rows:rows + EDGE, PAD:cols + PAD] = edge

    @pl.when(me_t == nt - 1)
    def _():
        d[1:cells + 1, rows + EDGE:, PAD:cols + PAD] = edge

    pl.semaphore_wait(barrier, nt - 1 + nd - 1)

    @pl.loop(0, nb)
    def _(b):
        for kind in range(4):
            @pl.when(sends[kind])
            def _():
                halo(kind, b).start()

    def label_copy(o):
        return pltpu.make_async_remote_copy(
            src_ref=names, dst_ref=arrived.at[o], send_sem=lsend.at[o], recv_sem=lrecv.at[o],
            device_id=(me_d, lax.rem(me_t + o, nt)), device_id_type=mesh_ids)

    own_labels = pltpu.make_async_copy(names, arrived.at[0], lsend.at[0])
    own_labels.start()

    @pl.loop(1, nt)
    def _(o):
        label_copy(o).start()

    @pl.loop(0, nt)
    def _(o):
        start = lax.rem(me_t + o, nt) * ppd
        first, last = ppd - 1, 0
        for p in range(ppd):
            h = home[p] - start
            hit = (h >= 0) & (h < ppd)
            first = jnp.where(hit, jnp.minimum(first, p), first)
            last = jnp.where(hit, p, last)
        route[o, 0] = first
        route[o, 1] = last

    def arrive(b):
        dens_copy(b).wait()
        for kind in range(4):
            @pl.when(gets[kind])
            def _():
                halo(kind, b).wait_recv()

    ascend = rank[0] == 0
    g_pair, dens_pair = (g0, g1), (dens0, dens1)
    facing = make_facing(d, g_pair, dens_pair, left, right, rows, zc)

    def depth_copy(k, b, src):
        to = lax.rem(me_d + k, nd)
        return pltpu.make_async_remote_copy(
            src_ref=out.at[:, pl.ds(pl.multiple_of(to * qrows, 8), qrows), cols_of(b)],
            dst_ref=recv.at[src, :, :, cols_of(b)],
            send_sem=dsend.at[b, k], recv_sem=drecv.at[b, src],
            device_id=(to, me_t), device_id_type=mesh_ids)

    def keep_own(b):
        mine = out[:, pl.ds(pl.multiple_of(me_d * qrows, 8), qrows), cols_of(b)]
        recv[me_d, :, :, cols_of(b)] = mine

    def brick(i, b):
        one, two = recv[i, 0, :, cols_of(b)], recv[i, 1, :, cols_of(b)]
        colors = jnp.stack([low_part(one), high_part(one), low_part(two)])
        return colors, high_part(two) * (1.0 / UNIT)

    def composite(b):
        for k in range(1, nd):
            depth_copy(k, b, lax.rem(me_d + k, nd)).wait_recv()
        color, trans = brick(0, b)
        for i in range(1, nd):
            new, new_trans = brick(i, b)
            front, back = jnp.where(ascend, color, new), jnp.where(ascend, new, color)
            color = front + jnp.where(ascend, trans, new_trans)[None] * back
            trans = trans * new_trans
        for ch in range(3):
            fin[ch, :, cols_of(b)] = coded(color[ch] + trans * (BACKDROP[ch] * UNIT))

    def tile_copy(o, part, window):
        return pltpu.make_async_remote_copy(
            src_ref=outbox.at[o, :, :, window], dst_ref=inbox.at[o, :, :, window],
            send_sem=tsend.at[part, o], recv_sem=trecv.at[part, o],
            device_id=(me_d, lax.rem(me_t + o, nt)), device_id_type=mesh_ids)

    def tile_own(part, window):
        return pltpu.make_async_copy(
            outbox.at[0, :, :, window], inbox.at[0, :, :, window], tsend.at[part, 0])

    def ship(part, window):
        def piece(p, r):
            if width == cols:
                return fin[:, pl.ds(p * rpp + r, 1), window]
            per = cols // width
            c = pl.multiple_of(lax.rem(p, per) * width, width)
            return fin[:, pl.ds(lax.div(p, per), 1), pl.ds(c, width)]

        @pl.loop(0, nt)
        def _(o):
            for r in range(rpp):
                outbox[o, :, r:r + 1, window] = join(piece(route[o, 0], r), piece(route[o, 1], r))

        tile_own(part, window).start()

        @pl.loop(1, nt)
        def _(o):
            tile_copy(o, part, window).start()

    arrive(0)
    arrive(1)

    @pl.loop(0, its)
    def _(it):
        facing(0, 0, it)

    def finish(b):
        composite(b)
        if groups == nb:
            ship(b, cols_of(b))

    def step(b, slot):
        @pl.when(b + 2 < nb)
        def _():
            arrive(b + 2)

        ahead = lax.rem(b + 1, nb)

        @pl.loop(0, its)
        def _(it):
            facing(ahead, 1 - slot, it)
            k = lax.div(it, parts) + 1
            part = lax.rem(it, parts)
            band = pl.multiple_of(lax.rem(me_d + k, nd) * qrows, 8)
            vals = march(dens_pair[slot], g_pair[slot], ascend, band,
                         pl.ds(pl.multiple_of(part * MC, MC), MC), qrows, cells)
            c0, c1, c2, tr = (coded(val * UNIT) for val in vals)
            lanes = pl.ds(pl.multiple_of(b * CB + part * MC, MC), MC)
            out[0, pl.ds(band, qrows), lanes] = join(c0, c1)
            out[1, pl.ds(band, qrows), lanes] = join(c2, tr)

            @pl.when((part == parts - 1) & (k < nd))
            def _():
                depth_copy(k, b, me_d).start()

        keep_own(b)

        @pl.when(b > 0)
        def _():
            finish(b - 1)

    @pl.loop(0, nb // 2)
    def _(pair):
        step(2 * pair, 0)
        step(2 * pair + 1, 1)

    finish(nb - 1)
    if groups != nb:
        ship(0, pl.ds(0, width))

    own_labels.wait()

    @pl.loop(1, nt)
    def _(o):
        label_copy(o).wait()

    @pl.loop(0, groups)
    def _(part):
        window = cols_of(part) if groups == nb else pl.ds(0, width)
        tile_own(part, window).wait()

        @pl.loop(1, nt)
        def _(o):
            tile_copy(o, part, window).wait()

    @pl.loop(0, nb)
    def _(b):
        for k in range(1, nd):
            depth_copy(k, b, me_d).wait_send()

    for kind in range(4):
        @pl.when(sends[kind])
        def _():
            @pl.loop(0, nb)
            def _(b):
                halo(kind, b).wait_send()


def place_kernel(arrived, inbox, display):
    nt, rpp, width = inbox.shape[0], inbox.shape[2], inbox.shape[3]
    ppd = display.shape[2]
    start = lax.axis_index("tile") * ppd

    @pl.loop(0, nt)
    def _(o):
        first, last = jnp.int32(NONE), jnp.int32(NONE)
        for p in range(ppd):
            h = arrived[o, 0, p] - start
            hit = (h >= 0) & (h < ppd)
            first = jnp.where(hit & (first == NONE), h, first)
            last = jnp.where(hit, h, last)

        def put(label, part):
            for r in range(rpp):
                piece = part(inbox[o, :, r:r + 1, :]) * (1.0 / UNIT)
                display[:, 0, pl.ds(label, 1), r * width:(r + 1) * width] = piece

        @pl.when(first != NONE)
        def _():
            put(first, low_part)

        @pl.when(last != first)
        def _():
            put(last, high_part)


def on_device(density, depth_rank, piece_home):
    cells, rows, cols = density.shape
    nd, nt = lax.axis_size("depth"), lax.axis_size("tile")
    ppd = piece_home.shape[0]
    qrows = rows // nd
    piece_len = qrows * cols // ppd
    width = min(piece_len, cols)
    rpp = piece_len // width
    nb = cols // CB
    groups = nb if width == cols else 1

    names = piece_home.reshape(1, ppd)
    left, right = stencils(rows)
    anyspec = pl.BlockSpec(memory_space=pl.ANY)
    vmem = pl.BlockSpec(memory_space=pltpu.VMEM)
    smem = pl.BlockSpec(memory_space=pltpu.SMEM)
    dma = pltpu.SemaphoreType.DMA
    f32, i32 = jnp.float32, jnp.int32
    inbox, arrived = pl.pallas_call(
        lambda *refs: brick_kernel(nd, nt, ppd, *refs),
        out_shape=(jax.ShapeDtypeStruct((nt, 3, rpp, width), i32),
                   jax.ShapeDtypeStruct((nt, 1, ppd), i32)),
        in_specs=[smem, smem] + [anyspec] * 2 + [vmem] * 2,
        out_specs=(anyspec, anyspec),
        scratch_shapes=[
            pltpu.VMEM((cells + 2, rows + 2 * EDGE, cols + 2 * PAD), jnp.bfloat16),
            pltpu.VMEM((cells, rows, CB), f32),
            pltpu.VMEM((cells, rows, CB), f32),
            pltpu.VMEM((cells, rows, CB), jnp.bfloat16),
            pltpu.VMEM((cells, rows, CB), jnp.bfloat16),
            pltpu.VMEM((2, rows, cols), i32),
            pltpu.VMEM((nd, 2, qrows, cols), i32),
            pltpu.VMEM((3, qrows, cols), i32),
            pltpu.VMEM((nt, 3, rpp, width), i32),
            pltpu.SMEM((nt, MOST), i32),
            dma((nb,)), dma((4, nb)), dma((4, nb)), dma((nb, nd)), dma((nb, nd)),
            dma((groups, nt)), dma((groups, nt)), dma((nt,)), dma((nt,)),
        ],
        compiler_params=pltpu.CompilerParams(
            collective_id=0, has_side_effects=True, vmem_limit_bytes=56 * 1024 * 1024),
    )(depth_rank, piece_home, density, names, left, right)
    return pl.pallas_call(
        place_kernel,
        out_shape=jax.ShapeDtypeStruct((3, 1, ppd, piece_len), f32),
        in_specs=[smem, vmem],
        out_specs=vmem,
    )(arrived, inbox)


def solution(mesh):
    in_specs = (P("depth", "tile", None), P(), P("tile"))
    out_specs = P(None, "depth", "tile", None)
    return jax.shard_map(
        on_device, mesh=mesh, in_specs=in_specs, out_specs=out_specs, check_vma=False
    )
```

time: 67.2 us -> 63.6 us (0.946)
  local copies, waits for them, and re-layouts: 2.82 us -> 0 us
  other arithmetic: 1.44 us -> 0 us
    slice x1 -> x0, local copies, waits for them, and re-layouts: 1.97 us -> none  [on_device(): ylast, yfirst = (density[:, rows - 1], density[:, 0])]
    squeeze x1 -> x0, local copies, waits for them, and re-layouts: 0.84 us -> none  [on_device(): ylast, yfirst = (density[:, rows - 1], density[:, 0])]
    reduce_max x1 -> x0, other arithmetic: 0.68 us -> none  [on_device(): jnp.max(jnp.where(goes, signs * code[None, None, None, :], EMPTY), axis=3)]
    select_n x2 -> x0, other arithmetic: 0.68 us -> none  [the longest x1 0.67 us: on_device(): offset = (owners - lax.axis_index('tile') + nt) % nt]
where the time goes in v1:
time: 63.6 us; the launch traced here: 63.5 us
  Pallas kernels  63.4 us (100%)
    pallas_call x1, Pallas kernels, on_device(): pl.pallas_call(lambda *refs: brick_kernel(nd, nt, ppd, *refs), out_shape=...  61.3 us
    pallas_call x1, Pallas kernels, on_device(): pl.pallas_call(place_kernel, out_shape=jax.ShapeDtypeStruct((3, 1, ppd, p...  2.17 us

profile of v1, /device:TPU:0, one launch (start us, length us, event | category | flops | bytes accessed | tf_op | source)
XLA Modules:
  0.0 63.5 jit_solution(10999461633092011696)
XLA Ops:
  0.0 61.3 %shard_map.55 = (s32[8,3,2,2048]{3,2,1,0:T(2,128)}, s32[8,1,8]{2,1,0:T(1,128)}) custom-call(s32[4]{0:T(128)} %refs_0_.1, s32[8]{0:T(128)} %refs_1_.1, bf16[32,64,2048]{2,1,0:T(8,128)(2,1)} %refs_2_.1, s32[1,8]{1,0:T(1,128)} %bitcast.1, bf16[64,208]{1,0:T(8,128)(2,1)} %constant.4.clone.refs_4_, bf16[512,256]{1,0:T(8,128)(2,1)} %constant.5.clone.refs_5_), custom_call_target="tpu_custom_call" | custom-call | tf_op jit(solution)/shard_map/pallas_call | solution.py:424
  61.3 2.2 %shard_map.56 = f32[3,1,8,4096]{3,2,1,0:T(8,128)} custom-call(s32[8,1,8]{2,1,0:T(1,128)} %get-tuple-element.7.arrived, s32[8,3,2,2048]{3,2,1,0:T(2,128)} %get-tuple-element.8.inbox), custom_call_target="tpu_custom_call" | custom-call | tf_op jit(solution)/shard_map/pallas_call | solution.py:447

commit v2 on v1

--- a/solution.py
+++ b/solution.py
@@ -49,36 +49,42 @@
     return jnp.asarray(left, jnp.bfloat16), jnp.asarray(right, jnp.bfloat16)
 
 
-def make_facing(d, g_pair, dens_pair, left, right, rows, zc):
-    def facing(block, slot, chunk):
-        z0 = chunk * zc
-        g, dens16 = g_pair[slot], dens_pair[slot]
+def make_facing(d, g, dens16, left, right, rows):
+    def begin(block, slot, z):
         c0 = pl.multiple_of(block * CB, CB)
         c1 = pl.multiple_of(block * CB + PAD, PAD)
-        wide = d[pl.ds(z0 + 1, zc), 0:rows, pl.ds(c0, CB + 2 * PAD)]
-        dx = jnp.dot(wide.reshape(zc * rows, CB + 2 * PAD), right[...],
-                     preferred_element_type=jnp.float32)
-        dens16[pl.ds(z0, zc)] = wide[:, :, PAD:PAD + CB]
-        for i in range(zc):
-            tall = jnp.concatenate([
-                d[z0 + i, 0:rows, pl.ds(c1, CB)],
-                d[z0 + i + 1, :, pl.ds(c1, CB)],
-                d[z0 + i + 2, 0:rows, pl.ds(c1, CB)]], axis=0)
-            dyz = jnp.dot(left[...], tall, preferred_element_type=jnp.float32)
-            g[z0 + i] = dyz + dx[i * rows:(i + 1) * rows]
-
-    return facing
-
-
-def march(dens16, g, ascend, r0, lanes, band_rows, cells):
+        wide = d[z + 1, 0:rows, pl.ds(c0, CB + 2 * PAD)]
+        tall = jnp.concatenate([
+            d[z, 0:rows, pl.ds(c1, CB)],
+            d[z + 1, :, pl.ds(c1, CB)],
+            d[z + 2, 0:rows, pl.ds(c1, CB)]], axis=0)
+        dx = jnp.dot(wide, right[...], preferred_element_type=jnp.float32)
+        both = dx + jnp.dot(left[...], tall, preferred_element_type=jnp.float32)
+        dens16[slot, z] = wide[:, PAD:PAD + CB]
+        return slot, z, both
+
+    def end(slot, z, both):
+        g[slot, z] = both
+
+    return begin, end
+
+
+def march(dens16, g, slot, ascend, r0, lanes, band_rows, cells, zc, begin, end):
     bias = (0.35 + 0.65 * 0.5) / (0.65 * 0.5)
     zero = jnp.zeros((band_rows, MC), jnp.float32)
     trans = zero + 1.0
     total = m0 = m1 = wave = zero
     for k in range(cells):
+        if k == 0:
+            held = begin(0)
+        turn = (k * 16 - 6 * cells) // (3 * cells)
+        if k * 16 == (6 + 3 * turn) * cells and 0 <= turn < zc:
+            end(*held)
+            if turn + 1 < zc:
+                held = begin(turn + 1)
         z = jnp.where(ascend, k, cells - 1 - k)
-        dens = dens16[z, pl.ds(r0, band_rows), lanes].astype(jnp.float32)
-        face = g[z, pl.ds(r0, band_rows), lanes]
+        dens = dens16[slot, z, pl.ds(r0, band_rows), lanes].astype(jnp.float32)
+        face = g[slot, z, pl.ds(r0, band_rows), lanes]
         shade = jnp.tanh(face * (0.5 * SHARPNESS * LIGHT_X)) + bias
         after = trans * jnp.exp2(dens * (-EXTINCT * math.log2(math.e)))
         ws = (trans - after) * shade
@@ -119,7 +125,7 @@
 
 
 def brick_kernel(nd, nt, ppd, rank, home, dens, names, left, right, inbox, arrived,
-                 d, g0, g1, dens0, dens1, out, recv, fin, outbox, route,
+                 d, g, dens16, out, recv, fin, outbox, route,
                  dens_sem, hsend, hrecv, dsend, drecv, tsend, trecv, lsend, lrecv):
     cells, rows, cols = dens.shape
     nb, parts = cols // CB, CB // MC
@@ -235,8 +241,7 @@
                 halo(kind, b).wait_recv()
 
     ascend = rank[0] == 0
-    g_pair, dens_pair = (g0, g1), (dens0, dens1)
-    facing = make_facing(d, g_pair, dens_pair, left, right, rows, zc)
+    begin, end = make_facing(d, g, dens16, left, right, rows)
 
     def depth_copy(k, b, src):
         to = lax.rem(me_d + k, nd)
@@ -301,14 +306,18 @@
 
     @pl.loop(0, its)
     def _(it):
-        facing(0, 0, it)
+        for i in range(zc):
+            end(*begin(0, 0, it * zc + i))
 
     def finish(b):
         composite(b)
         if groups == nb:
             ship(b, cols_of(b))
 
-    def step(b, slot):
+    @pl.loop(0, nb)
+    def _(b):
+        slot = lax.rem(b, 2)
+
         @pl.when(b + 2 < nb)
         def _():
             arrive(b + 2)
@@ -317,12 +326,12 @@
 
         @pl.loop(0, its)
         def _(it):
-            facing(ahead, 1 - slot, it)
             k = lax.div(it, parts) + 1
             part = lax.rem(it, parts)
             band = pl.multiple_of(lax.rem(me_d + k, nd) * qrows, 8)
-            vals = march(dens_pair[slot], g_pair[slot], ascend, band,
-                         pl.ds(pl.multiple_of(part * MC, MC), MC), qrows, cells)
+            vals = march(dens16, g, slot, ascend, band,
+                         pl.ds(pl.multiple_of(part * MC, MC), MC), qrows, cells, zc,
+                         lambda i: begin(ahead, 1 - slot, it * zc + i), end)
             c0, c1, c2, tr = (coded(val * UNIT) for val in vals)
             lanes = pl.ds(pl.multiple_of(b * CB + part * MC, MC), MC)
             out[0, pl.ds(band, qrows), lanes] = join(c0, c1)
@@ -337,11 +346,6 @@
         @pl.when(b > 0)
         def _():
             finish(b - 1)
-
-    @pl.loop(0, nb // 2)
-    def _(pair):
-        step(2 * pair, 0)
-        step(2 * pair + 1, 1)
 
     finish(nb - 1)
     if groups != nb:
@@ -429,10 +433,8 @@
         out_specs=(anyspec, anyspec),
         scratch_shapes=[
             pltpu.VMEM((cells + 2, rows + 2 * EDGE, cols + 2 * PAD), jnp.bfloat16),
-            pltpu.VMEM((cells, rows, CB), f32),
-            pltpu.VMEM((cells, rows, CB), f32),
-            pltpu.VMEM((cells, rows, CB), jnp.bfloat16),
-            pltpu.VMEM((cells, rows, CB), jnp.bfloat16),
+            pltpu.VMEM((2, cells, rows, CB), f32),
+            pltpu.VMEM((2, cells, rows, CB), jnp.bfloat16),
             pltpu.VMEM((2, rows, cols), i32),
             pltpu.VMEM((nd, 2, qrows, cols), i32),
             pltpu.VMEM((3, qrows, cols), i32),

time: 63.6 us -> 59 us (0.928)
  Pallas kernels: 63.4 us -> 58.9 us
    pallas_call x1, Pallas kernels: 61.3 us -> 56.7 us  [on_device(): pl.pallas_call(lambda *refs: brick_kernel(nd, nt, ppd, *refs), out_shape=...]
where the time goes in v2:
time: 59 us; the launch traced here: 58.9 us
  Pallas kernels  58.9 us (100%)
    pallas_call x1, Pallas kernels, on_device(): pl.pallas_call(lambda *refs: brick_kernel(nd, nt, ppd, *refs), out_shape=...  56.7 us
    pallas_call x1, Pallas kernels, on_device(): pl.pallas_call(place_kernel, out_shape=jax.ShapeDtypeStruct((3, 1, ppd, p...  2.17 us

profile of v2, /device:TPU:0, one launch (start us, length us, event | category | flops | bytes accessed | tf_op | source)
XLA Modules:
  0.0 58.9 jit_solution(4898681408843973034)
XLA Ops:
  0.0 56.7 %shard_map.55 = (s32[8,3,2,2048]{3,2,1,0:T(2,128)}, s32[8,1,8]{2,1,0:T(1,128)}) custom-call(s32[4]{0:T(128)} %refs_0_.1, s32[8]{0:T(128)} %refs_1_.1, bf16[32,64,2048]{2,1,0:T(8,128)(2,1)} %refs_2_.1, s32[1,8]{1,0:T(1,128)} %bitcast.1, bf16[64,208]{1,0:T(8,128)(2,1)} %constant.4.clone.refs_4_, bf16[512,256]{1,0:T(8,128)(2,1)} %constant.5.clone.refs_5_), custom_call_target="tpu_custom_call" | custom-call | tf_op jit(solution)/shard_map/pallas_call | solution.py:428
  56.7 2.2 %shard_map.56 = f32[3,1,8,4096]{3,2,1,0:T(8,128)} custom-call(s32[8,1,8]{2,1,0:T(1,128)} %get-tuple-element.7.arrived, s32[8,3,2,2048]{3,2,1,0:T(2,128)} %get-tuple-element.8.inbox), custom_call_target="tpu_custom_call" | custom-call | tf_op jit(solution)/shard_map/pallas_call | solution.py:449

commit v3 on v2

--- a/solution.py
+++ b/solution.py
@@ -49,39 +49,37 @@
     return jnp.asarray(left, jnp.bfloat16), jnp.asarray(right, jnp.bfloat16)
 
 
-def make_facing(d, g, dens16, left, right, rows):
-    def begin(block, slot, z):
-        c0 = pl.multiple_of(block * CB, CB)
+def make_facing(d, g, dens16, left, right, rows, zc):
+    def across(block, chunk):
+        wide = d[pl.ds(chunk * zc + 1, zc), 0:rows, pl.ds(pl.multiple_of(block * CB, CB), CB + 2 * PAD)]
+        wide = wide.reshape(zc * rows, CB + 2 * PAD)
+        return [jnp.dot(wide[:, h:h + CB], right[h:h + CB], preferred_element_type=jnp.float32)
+                for h in range(0, CB + 2 * PAD, CB)]
+
+    def begin(block, chunk, i):
+        z = chunk * zc + i
         c1 = pl.multiple_of(block * CB + PAD, PAD)
-        wide = d[z + 1, 0:rows, pl.ds(c0, CB + 2 * PAD)]
         tall = jnp.concatenate([
             d[z, 0:rows, pl.ds(c1, CB)],
             d[z + 1, :, pl.ds(c1, CB)],
             d[z + 2, 0:rows, pl.ds(c1, CB)]], axis=0)
-        dx = jnp.dot(wide, right[...], preferred_element_type=jnp.float32)
-        both = dx + jnp.dot(left[...], tall, preferred_element_type=jnp.float32)
-        dens16[slot, z] = wide[:, PAD:PAD + CB]
-        return slot, z, both
-
-    def end(slot, z, both):
-        g[slot, z] = both
-
-    return begin, end
-
-
-def march(dens16, g, slot, ascend, r0, lanes, band_rows, cells, zc, begin, end):
+        return jnp.dot(left[...], tall, preferred_element_type=jnp.float32)
+
+    def end(block, slot, chunk, i, dx, dyz):
+        z = chunk * zc + i
+        g[slot, z] = dyz + sum(part[i * rows:(i + 1) * rows] for part in dx)
+        dens16[slot, z] = d[z + 1, 0:rows, pl.ds(pl.multiple_of(block * CB + PAD, PAD), CB)]
+
+    return across, begin, end
+
+
+def march(dens16, g, slot, ascend, r0, lanes, band_rows, cells, beside):
     bias = (0.35 + 0.65 * 0.5) / (0.65 * 0.5)
     zero = jnp.zeros((band_rows, MC), jnp.float32)
     trans = zero + 1.0
     total = m0 = m1 = wave = zero
     for k in range(cells):
-        if k == 0:
-            held = begin(0)
-        turn = (k * 16 - 6 * cells) // (3 * cells)
-        if k * 16 == (6 + 3 * turn) * cells and 0 <= turn < zc:
-            end(*held)
-            if turn + 1 < zc:
-                held = begin(turn + 1)
+        beside(k)
         z = jnp.where(ascend, k, cells - 1 - k)
         dens = dens16[slot, z, pl.ds(r0, band_rows), lanes].astype(jnp.float32)
         face = g[slot, z, pl.ds(r0, band_rows), lanes]
@@ -108,6 +106,27 @@
     )
 
 
+class Beside:
+    def __init__(self, steps, planes, across, begin, end):
+        self.across, self.begin, self.end = across, begin, end
+        gap = steps // planes
+        self.turns = {}
+        for i in range(planes):
+            self.turns.setdefault(i * gap, []).append((True, i))
+            stop = min(i * gap + gap * 24 // 8, steps)
+            self.turns.setdefault(stop, []).append((False, i))
+        self.held, self.dx = {}, None
+
+    def __call__(self, step):
+        if step == 0:
+            self.dx = self.across()
+        for fresh, i in self.turns.get(step, ()):
+            if fresh:
+                self.held[i] = self.begin(i)
+            else:
+                self.end(i, self.dx, self.held[i])
+
+
 def coded(value):
     return jnp.clip(value + 0.5, 0.0, UNIT).astype(jnp.int32)
 
@@ -129,8 +148,7 @@
                  dens_sem, hsend, hrecv, dsend, drecv, tsend, trecv, lsend, lrecv):
     cells, rows, cols = dens.shape
     nb, parts = cols // CB, CB // MC
-    its = nd * parts
-    zc = cells // its
+    zc = cells // nd
     qrows = rows // nd
     width, rpp = outbox.shape[3], outbox.shape[2]
     groups = tsend.shape[0]
@@ -235,13 +253,15 @@
 
     def arrive(b):
         dens_copy(b).wait()
+
+    def arrive_halo(b):
         for kind in range(4):
             @pl.when(gets[kind])
             def _():
                 halo(kind, b).wait_recv()
 
     ascend = rank[0] == 0
-    begin, end = make_facing(d, g, dens16, left, right, rows)
+    across, begin, end = make_facing(d, g, dens16, left, right, rows, zc)
 
     def depth_copy(k, b, src):
         to = lax.rem(me_d + k, nd)
@@ -303,11 +323,13 @@
 
     arrive(0)
     arrive(1)
-
-    @pl.loop(0, its)
+    arrive_halo(0)
+
+    @pl.loop(0, nd)
     def _(it):
+        dx = across(0, it)
         for i in range(zc):
-            end(*begin(0, 0, it * zc + i))
+            end(0, 0, it, i, dx, begin(0, it, i))
 
     def finish(b):
         composite(b)
@@ -322,22 +344,28 @@
         def _():
             arrive(b + 2)
 
+        @pl.when(b + 1 < nb)
+        def _():
+            arrive_halo(b + 1)
+
         ahead = lax.rem(b + 1, nb)
 
-        @pl.loop(0, its)
+        @pl.loop(0, nd)
         def _(it):
-            k = lax.div(it, parts) + 1
-            part = lax.rem(it, parts)
+            k = it + 1
             band = pl.multiple_of(lax.rem(me_d + k, nd) * qrows, 8)
-            vals = march(dens16, g, slot, ascend, band,
-                         pl.ds(pl.multiple_of(part * MC, MC), MC), qrows, cells, zc,
-                         lambda i: begin(ahead, 1 - slot, it * zc + i), end)
-            c0, c1, c2, tr = (coded(val * UNIT) for val in vals)
-            lanes = pl.ds(pl.multiple_of(b * CB + part * MC, MC), MC)
-            out[0, pl.ds(band, qrows), lanes] = join(c0, c1)
-            out[1, pl.ds(band, qrows), lanes] = join(c2, tr)
-
-            @pl.when((part == parts - 1) & (k < nd))
+            beside = Beside(parts * cells, zc, lambda: across(ahead, it), lambda i: begin(ahead, it, i),
+                            lambda i, dx, dyz: end(ahead, 1 - slot, it, i, dx, dyz))
+            for part in range(parts):
+                vals = march(dens16, g, slot, ascend, band, slice(part * MC, (part + 1) * MC), qrows, cells,
+                             lambda step, first=part * cells: beside(first + step))
+                c0, c1, c2, tr = (coded(val * UNIT) for val in vals)
+                lanes = pl.ds(pl.multiple_of(b * CB + part * MC, MC), MC)
+                out[0, pl.ds(band, qrows), lanes] = join(c0, c1)
+                out[1, pl.ds(band, qrows), lanes] = join(c2, tr)
+            beside(parts * cells)
+
+            @pl.when(k < nd)
             def _():
                 depth_copy(k, b, me_d).start()
 

time: 59 us -> 54.8 us (0.929)
  Pallas kernels: 58.9 us -> 54.6 us
    pallas_call x1, Pallas kernels: 56.7 us -> 52.5 us  [on_device(): pl.pallas_call(lambda *refs: brick_kernel(nd, nt, ppd, *refs), out_shape=...]
where the time goes in v3:
time: 54.8 us; the launch traced here: 54.6 us
  Pallas kernels  54.6 us (100%)
    pallas_call x1, Pallas kernels, on_device(): pl.pallas_call(lambda *refs: brick_kernel(nd, nt, ppd, *refs), out_shape=...  52.5 us
    pallas_call x1, Pallas kernels, on_device(): pl.pallas_call(place_kernel, out_shape=jax.ShapeDtypeStruct((3, 1, ppd, p...  2.17 us

profile of v3, /device:TPU:0, one launch (start us, length us, event | category | flops | bytes accessed | tf_op | source)
XLA Modules:
  0.0 54.6 jit_solution(6639418196404892525)
XLA Ops:
  0.0 52.5 %shard_map.55 = (s32[8,3,2,2048]{3,2,1,0:T(2,128)}, s32[8,1,8]{2,1,0:T(1,128)}) custom-call(s32[4]{0:T(128)} %refs_0_.1, s32[8]{0:T(128)} %refs_1_.1, bf16[32,64,2048]{2,1,0:T(8,128)(2,1)} %refs_2_.1, s32[1,8]{1,0:T(1,128)} %bitcast.1, bf16[64,208]{1,0:T(8,128)(2,1)} %constant.4.clone.refs_4_, bf16[512,256]{1,0:T(8,128)(2,1)} %constant.5.clone.refs_5_), custom_call_target="tpu_custom_call" | custom-call | tf_op jit(solution)/shard_map/pallas_call | solution.py:456
  52.5 2.2 %shard_map.56 = f32[3,1,8,4096]{3,2,1,0:T(8,128)} custom-call(s32[8,1,8]{2,1,0:T(1,128)} %get-tuple-element.7.arrived, s32[8,3,2,2048]{3,2,1,0:T(2,128)} %get-tuple-element.8.inbox), custom_call_target="tpu_custom_call" | custom-call | tf_op jit(solution)/shard_map/pallas_call | solution.py:477

commit v4 on v3

--- a/solution.py
+++ b/solution.py
@@ -46,10 +46,11 @@
     for c in range(CB):
         right[c + PAD + 1, c] = 1.0
         right[c + PAD - 1, c] = -1.0
-    return jnp.asarray(left, jnp.bfloat16), jnp.asarray(right, jnp.bfloat16)
-
-
-def make_facing(d, g, dens16, left, right, rows, zc):
+    plain = np.delete(left, np.s_[2 * rows:2 * rows + 2 * EDGE], axis=1)
+    return [jnp.asarray(m, jnp.bfloat16) for m in (left, plain, right)]
+
+
+def make_facing(d, g, dens16, left, plain, right, rows, cells, zc):
     def across(block, chunk):
         wide = d[pl.ds(chunk * zc + 1, zc), 0:rows, pl.ds(pl.multiple_of(block * CB, CB), CB + 2 * PAD)]
         wide = wide.reshape(zc * rows, CB + 2 * PAD)
@@ -70,7 +71,38 @@
         g[slot, z] = dyz + sum(part[i * rows:(i + 1) * rows] for part in dx)
         dens16[slot, z] = d[z + 1, 0:rows, pl.ds(pl.multiple_of(block * CB + PAD, PAD), CB)]
 
-    return across, begin, end
+    def inner(block, z):
+        c1 = pl.multiple_of(block * CB + PAD, PAD)
+        tall = d[pl.ds(z, 3), 0:rows, pl.ds(c1, CB)].reshape(3 * rows, CB)
+        wide = d[z + 1, 0:rows, pl.ds(pl.multiple_of(block * CB, CB), CB + 2 * PAD)]
+        dx = jnp.dot(wide, right[...], preferred_element_type=jnp.float32)
+        g[0, z] = jnp.dot(plain[...], tall, preferred_element_type=jnp.float32) + dx
+        dens16[0, z] = d[z + 1, 0:rows, pl.ds(c1, CB)]
+
+    def early(block):
+        @pl.loop(0, cells // 2 - 1)
+        def _(i):
+            for j in range(2):
+                inner(block, 2 * i + 1 + j)
+
+    def late(block):
+        wy = LIGHT_Y / LIGHT_X
+        c1 = pl.multiple_of(block * CB + PAD, PAD)
+        for z in (0, cells - 1):
+            inner(block, z)
+
+        @pl.loop(0, cells // 4)
+        def _(i):
+            sub = lax.broadcasted_iota(jnp.int32, (EDGE, CB), 0)
+            for j in range(4):
+                z = 4 * i + j
+                low = d[z + 1, rows:rows + EDGE, pl.ds(c1, CB)].astype(jnp.float32)
+                high = d[z + 1, rows + EDGE:, pl.ds(c1, CB)].astype(jnp.float32)
+                g[0, z, 0:EDGE] = g[0, z, 0:EDGE] - jnp.where(sub == 0, pltpu.roll(low, 1, 0), 0.0) * wy
+                g[0, z, rows - EDGE:] = g[0, z, rows - EDGE:] + jnp.where(
+                    sub == EDGE - 1, pltpu.roll(high, EDGE - 1, 0), 0.0) * wy
+
+    return across, begin, end, early, late
 
 
 def march(dens16, g, slot, ascend, r0, lanes, band_rows, cells, beside):
@@ -143,7 +175,7 @@
     return lax.shift_right_logical(word, 16).astype(jnp.float32)
 
 
-def brick_kernel(nd, nt, ppd, rank, home, dens, names, left, right, inbox, arrived,
+def brick_kernel(nd, nt, ppd, rank, home, dens, names, left, plain, right, inbox, arrived,
                  d, g, dens16, out, recv, fin, outbox, route,
                  dens_sem, hsend, hrecv, dsend, drecv, tsend, trecv, lsend, lrecv):
     cells, rows, cols = dens.shape
@@ -192,8 +224,7 @@
     sends = (me_d < nd - 1, me_d > 0, me_t < nt - 1, me_t > 0)
     gets = (me_d > 0, me_d < nd - 1, me_t > 0, me_t < nt - 1)
 
-    @pl.loop(0, nb)
-    def _(b):
+    for b in range(2):
         dens_copy(b).start()
 
     side = jnp.zeros((cells + 2, rows + 2 * EDGE, PAD), d.dtype)
@@ -220,12 +251,16 @@
 
     pl.semaphore_wait(barrier, nt - 1 + nd - 1)
 
-    @pl.loop(0, nb)
-    def _(b):
+    def send_halo(b):
         for kind in range(4):
             @pl.when(sends[kind])
             def _():
                 halo(kind, b).start()
+
+    send_halo(0)
+    dens_copy(2).start()
+    dens_copy(3).start()
+    send_halo(1)
 
     def label_copy(o):
         return pltpu.make_async_remote_copy(
@@ -261,7 +296,7 @@
                 halo(kind, b).wait_recv()
 
     ascend = rank[0] == 0
-    across, begin, end = make_facing(d, g, dens16, left, right, rows, zc)
+    across, begin, end, early, late = make_facing(d, g, dens16, left, plain, right, rows, cells, zc)
 
     def depth_copy(k, b, src):
         to = lax.rem(me_d + k, nd)
@@ -323,39 +358,37 @@
 
     arrive(0)
     arrive(1)
+    early(0)
     arrive_halo(0)
-
-    @pl.loop(0, nd)
-    def _(it):
-        dx = across(0, it)
-        for i in range(zc):
-            end(0, 0, it, i, dx, begin(0, it, i))
+    late(0)
 
     def finish(b):
         composite(b)
         if groups == nb:
             ship(b, cols_of(b))
 
-    @pl.loop(0, nb)
-    def _(b):
+    def block(b, beside_of):
         slot = lax.rem(b, 2)
 
-        @pl.when(b + 2 < nb)
-        def _():
-            arrive(b + 2)
-
-        @pl.when(b + 1 < nb)
-        def _():
+        if isinstance(b, int):
+            assert b == nb - 1
+        else:
+            @pl.when(b + 4 < nb)
+            def _():
+                dens_copy(b + 4).start()
+
+            @pl.when(b + 2 < nb)
+            def _():
+                send_halo(b + 2)
+                arrive(b + 2)
+
             arrive_halo(b + 1)
-
-        ahead = lax.rem(b + 1, nb)
 
         @pl.loop(0, nd)
         def _(it):
             k = it + 1
             band = pl.multiple_of(lax.rem(me_d + k, nd) * qrows, 8)
-            beside = Beside(parts * cells, zc, lambda: across(ahead, it), lambda i: begin(ahead, it, i),
-                            lambda i, dx, dyz: end(ahead, 1 - slot, it, i, dx, dyz))
+            beside = beside_of(b + 1, 1 - slot, it)
             for part in range(parts):
                 vals = march(dens16, g, slot, ascend, band, slice(part * MC, (part + 1) * MC), qrows, cells,
                              lambda step, first=part * cells: beside(first + step))
@@ -375,6 +408,15 @@
         def _():
             finish(b - 1)
 
+    def slopes_of(ahead, slot, it):
+        return Beside(parts * cells, zc, lambda: across(ahead, it), lambda i: begin(ahead, it, i),
+                      lambda i, dx, dyz: end(ahead, slot, it, i, dx, dyz))
+
+    @pl.loop(0, nb - 1)
+    def _(b):
+        block(b, slopes_of)
+
+    block(nb - 1, lambda ahead, slot, it: lambda step: None)
     finish(nb - 1)
     if groups != nb:
         ship(0, pl.ds(0, width))
@@ -447,7 +489,7 @@
     groups = nb if width == cols else 1
 
     names = piece_home.reshape(1, ppd)
-    left, right = stencils(rows)
+    left, plain, right = stencils(rows)
     anyspec = pl.BlockSpec(memory_space=pl.ANY)
     vmem = pl.BlockSpec(memory_space=pltpu.VMEM)
     smem = pl.BlockSpec(memory_space=pltpu.SMEM)
@@ -457,7 +499,7 @@
         lambda *refs: brick_kernel(nd, nt, ppd, *refs),
         out_shape=(jax.ShapeDtypeStruct((nt, 3, rpp, width), i32),
                    jax.ShapeDtypeStruct((nt, 1, ppd), i32)),
-        in_specs=[smem, smem] + [anyspec] * 2 + [vmem] * 2,
+        in_specs=[smem, smem] + [anyspec] * 2 + [vmem] * 3,
         out_specs=(anyspec, anyspec),
         scratch_shapes=[
             pltpu.VMEM((cells + 2, rows + 2 * EDGE, cols + 2 * PAD), jnp.bfloat16),
@@ -473,7 +515,7 @@
         ],
         compiler_params=pltpu.CompilerParams(
             collective_id=0, has_side_effects=True, vmem_limit_bytes=56 * 1024 * 1024),
-    )(depth_rank, piece_home, density, names, left, right)
+    )(depth_rank, piece_home, density, names, left, plain, right)
     return pl.pallas_call(
         place_kernel,
         out_shape=jax.ShapeDtypeStruct((3, 1, ppd, piece_len), f32),

time: 54.8 us -> 52.6 us (0.960)
  Pallas kernels: 54.6 us -> 52.4 us
    pallas_call x1, Pallas kernels: 52.5 us -> 50.2 us  [on_device(): pl.pallas_call(lambda *refs: brick_kernel(nd, nt, ppd, *refs), out_shape=...]
where the time goes in v4:
time: 52.6 us; the launch traced here: 52.4 us
  Pallas kernels  52.4 us (100%)
    pallas_call x1, Pallas kernels, on_device(): pl.pallas_call(lambda *refs: brick_kernel(nd, nt, ppd, *refs), out_shape=...  50.2 us
    pallas_call x1, Pallas kernels, on_device(): pl.pallas_call(place_kernel, out_shape=jax.ShapeDtypeStruct((3, 1, ppd, p...  2.17 us

profile of v4, /device:TPU:0, one launch (start us, length us, event | category | flops | bytes accessed | tf_op | source)
XLA Modules:
  0.0 52.4 jit_solution(1436495807341141182)
XLA Ops:
  0.0 50.2 %shard_map.64 = (s32[8,3,2,2048]{3,2,1,0:T(2,128)}, s32[8,1,8]{2,1,0:T(1,128)}) custom-call(s32[4]{0:T(128)} %refs_0_.1, s32[8]{0:T(128)} %refs_1_.1, bf16[32,64,2048]{2,1,0:T(8,128)(2,1)} %refs_2_.1, s32[1,8]{1,0:T(1,128)} %bitcast.1, bf16[64,208]{1,0:T(8,128)(2,1)} %constant.6.clone.refs_4_, bf16[64,192]{1,0:T(8,128)(2,1)} %constant.7.clone.refs_5_, ...), custom_call_target="tpu_custom_call" | custom-call | tf_op jit(solution)/shard_map/pallas_call | solution.py:498
  50.2 2.2 %shard_map.65 = f32[3,1,8,4096]{3,2,1,0:T(8,128)} custom-call(s32[8,1,8]{2,1,0:T(1,128)} %get-tuple-element.7.arrived, s32[8,3,2,2048]{3,2,1,0:T(2,128)} %get-tuple-element.8.inbox), custom_call_target="tpu_custom_call" | custom-call | tf_op jit(solution)/shard_map/pallas_call | solution.py:519

commit v5 on v4

--- a/solution.py
+++ b/solution.py
@@ -145,7 +145,7 @@
         self.turns = {}
         for i in range(planes):
             self.turns.setdefault(i * gap, []).append((True, i))
-            stop = min(i * gap + gap * 24 // 8, steps)
+            stop = min(i * gap + gap * 32 // 8, steps)
             self.turns.setdefault(stop, []).append((False, i))
         self.held, self.dx = {}, None
 

time: 52.6 us -> 52 us (0.989)
  Pallas kernels: 52.4 us -> 51.8 us
    pallas_call x1, Pallas kernels: 50.2 us -> 49.6 us  [on_device(): pl.pallas_call(lambda *refs: brick_kernel(nd, nt, ppd, *refs), out_shape=...]
where the time goes in v5:
time: 52 us; the launch traced here: 51.8 us
  Pallas kernels  51.8 us (100%)
    pallas_call x1, Pallas kernels, on_device(): pl.pallas_call(lambda *refs: brick_kernel(nd, nt, ppd, *refs), out_shape=...  49.6 us
    pallas_call x1, Pallas kernels, on_device(): pl.pallas_call(place_kernel, out_shape=jax.ShapeDtypeStruct((3, 1, ppd, p...  2.17 us

profile of v5, /device:TPU:0, one launch (start us, length us, event | category | flops | bytes accessed | tf_op | source)
XLA Modules:
  0.0 51.8 jit_solution(12615525876694585840)
XLA Ops:
  0.0 49.6 %shard_map.64 = (s32[8,3,2,2048]{3,2,1,0:T(2,128)}, s32[8,1,8]{2,1,0:T(1,128)}) custom-call(s32[4]{0:T(128)} %refs_0_.1, s32[8]{0:T(128)} %refs_1_.1, bf16[32,64,2048]{2,1,0:T(8,128)(2,1)} %refs_2_.1, s32[1,8]{1,0:T(1,128)} %bitcast.1, bf16[64,208]{1,0:T(8,128)(2,1)} %constant.6.clone.refs_4_, bf16[64,192]{1,0:T(8,128)(2,1)} %constant.7.clone.refs_5_, ...), custom_call_target="tpu_custom_call" | custom-call | tf_op jit(solution)/shard_map/pallas_call | solution.py:498
  49.7 2.2 %shard_map.65 = f32[3,1,8,4096]{3,2,1,0:T(8,128)} custom-call(s32[8,1,8]{2,1,0:T(1,128)} %get-tuple-element.7.arrived, s32[8,3,2,2048]{3,2,1,0:T(2,128)} %get-tuple-element.8.inbox), custom_call_target="tpu_custom_call" | custom-call | tf_op jit(solution)/shard_map/pallas_call | solution.py:519

commit v6 on v5

--- a/solution.py
+++ b/solution.py
@@ -387,6 +387,11 @@
         @pl.loop(0, nd)
         def _(it):
             k = it + 1
+
+            @pl.when((k == nd) & (b > 0))
+            def _():
+                finish(b - 1)
+
             band = pl.multiple_of(lax.rem(me_d + k, nd) * qrows, 8)
             beside = beside_of(b + 1, 1 - slot, it)
             for part in range(parts):
@@ -403,10 +408,6 @@
                 depth_copy(k, b, me_d).start()
 
         keep_own(b)
-
-        @pl.when(b > 0)
-        def _():
-            finish(b - 1)
 
     def slopes_of(ahead, slot, it):
         return Beside(parts * cells, zc, lambda: across(ahead, it), lambda i: begin(ahead, it, i),

time: 52 us -> 53.7 us (1.033)
  Pallas kernels: 51.8 us -> 53.5 us
    pallas_call x1, Pallas kernels: 49.6 us -> 51.4 us  [on_device(): pl.pallas_call(lambda *refs: brick_kernel(nd, nt, ppd, *refs), out_shape=...]
where the time goes in v6:
time: 53.7 us; the launch traced here: 53.5 us
  Pallas kernels  53.5 us (100%)
    pallas_call x1, Pallas kernels, on_device(): pl.pallas_call(lambda *refs: brick_kernel(nd, nt, ppd, *refs), out_shape=...  51.4 us
    pallas_call x1, Pallas kernels, on_device(): pl.pallas_call(place_kernel, out_shape=jax.ShapeDtypeStruct((3, 1, ppd, p...  2.17 us

profile of v6, /device:TPU:0, one launch (start us, length us, event | category | flops | bytes accessed | tf_op | source)
XLA Modules:
  0.0 53.5 jit_solution(6034101884607367350)
XLA Ops:
  0.0 51.4 %shard_map.64 = (s32[8,3,2,2048]{3,2,1,0:T(2,128)}, s32[8,1,8]{2,1,0:T(1,128)}) custom-call(s32[4]{0:T(128)} %refs_0_.1, s32[8]{0:T(128)} %refs_1_.1, bf16[32,64,2048]{2,1,0:T(8,128)(2,1)} %refs_2_.1, s32[1,8]{1,0:T(1,128)} %bitcast.1, bf16[64,208]{1,0:T(8,128)(2,1)} %constant.6.clone.refs_4_, bf16[64,192]{1,0:T(8,128)(2,1)} %constant.7.clone.refs_5_, ...), custom_call_target="tpu_custom_call" | custom-call | tf_op jit(solution)/shard_map/pallas_call | solution.py:499
  51.4 2.2 %shard_map.65 = f32[3,1,8,4096]{3,2,1,0:T(8,128)} custom-call(s32[8,1,8]{2,1,0:T(1,128)} %get-tuple-element.7.arrived, s32[8,3,2,2048]{3,2,1,0:T(2,128)} %get-tuple-element.8.inbox), custom_call_target="tpu_custom_call" | custom-call | tf_op jit(solution)/shard_map/pallas_call | solution.py:520
